TPU v7x, 512 devices: a whole 4x8x8 slice. The times are simulated.
512 devices in a mesh: blk: 8 (over y_lo, core), team: 64 (over y_hi, x, z).
Axes of the slice: x: 4, y: 8 (y_hi: 2, y_lo: 4; y = y_hi * 4 + y_lo), z: 8, core: 2. Of those that a mesh axis runs over, the one named last changes fastest.
Arguments:
- features: bfloat16 [65536, 256], P(('blk', 'team')), may hold values from -6 to 6
- weight: bfloat16 [256, 256], replicated, may hold values from -0.375 to 0.375
- bias: float32 [256], replicated, may hold values from -3 to 3
- cotangent: bfloat16 [65536, 256], P(('blk', 'team')), may hold values from -6 to 6
- adj_cols: int32 [64, 8, 8, 12], P('team', None, 'blk'), may hold values from 0 to 63, as said below
- adj_vals: bfloat16 [64, 8, 8, 12, 128, 128], P('team', None, 'blk'), as said below
Outputs:
- hidden: bfloat16 [65536, 256], P(('blk', 'team'))
- grad_input: bfloat16 [65536, 256], P(('blk', 'team'))
- grad_weight: float32 [256, 256], replicated
- grad_bias: float32 [256], replicated
Inputs may be any that keep to these rules, and one draw needn't show every extreme that they name: `adj_cols`: for every node panel and column group the 12 entries are distinct. Block (i, j) of A is listed exactly when block (j, i) is, every column panel is listed by exactly 12 row panels of each column group, and A is symmetric. `adj_vals`: the block listed for panels (i, j) is the transpose of the block listed for (j, i), so A is symmetric.
All inputs are finite; a program needn't handle non-finite values.
Results may differ from a plain program's by a relative error of at most 0.0075.
Values may be sent and summed in bfloat16 or wider, within the bound.
No kernel may reach another device: no remote copies, remote signals or barrier semaphores. Data moves between devices by JAX's collectives and lax.ppermute only.
A program may use at most 64 MiB of HBM per device.

v0:
```python
import jax
import jax.numpy as jnp
from jax import lax
from jax.sharding import Mesh
from jax.sharding import PartitionSpec as P

BLK_AXES = ("y_lo", "core")
TEAM_AXES = ("y_hi", "x", "z")
PLANE = ("x", "z")
ALL_AXES = BLK_AXES + TEAM_AXES


def fine_mesh(mesh):
    blk = mesh.shape["blk"]
    team = mesh.shape["team"]
    sizes = (blk // 2, 2, 2, 4, team // 8)
    return Mesh(mesh.devices.reshape(sizes), ALL_AXES)


def gather_team(rows):
    other = lax.ppermute(rows, "y_hi", perm=[(0, 1), (1, 0)])
    pair = jnp.stack([rows, other], axis=0)
    full = lax.all_gather(pair, PLANE, axis=0, tiled=True)
    return full.reshape(-1, rows.shape[1])


def member_slots(members, plane_size):
    my_hi = lax.axis_index("y_hi")
    return members % plane_size * 2 + (members // plane_size != my_hi).astype(jnp.int32)


def collect(panels, slots, adj_vals):
    block = adj_vals.shape[-1]
    width = panels.shape[1]
    stacked = panels.reshape(panels.shape[0] // block, block, width)
    picked = jnp.take(stacked, slots, axis=0)
    summed = jnp.einsum(
        "rkij,rkjf->rif", adj_vals[0, :, 0], picked, preferred_element_type=jnp.float32
    )
    return summed.reshape(-1, width)


def activation(value):
    return jax.nn.gelu(value, approximate=True)


def local(features, weight, bias, cotangent, adj_cols, adj_vals):
    plane_size = lax.psum(1, PLANE)
    slots = member_slots(adj_cols[0, :, 0, :], plane_size)
    product = jnp.dot(features, weight, preferred_element_type=jnp.float32).astype(jnp.bfloat16)
    gathered = gather_team(product)
    partial_rows = collect(gathered, slots, adj_vals)
    summed = lax.psum_scatter(partial_rows, BLK_AXES, scatter_dimension=0, tiled=True)
    pre = summed + bias[None, :]
    activated, pullback = jax.vjp(activation, pre)
    hidden = activated.astype(jnp.bfloat16)
    pulled = pullback(cotangent.astype(jnp.float32))[0].astype(jnp.bfloat16)
    pulled_group = gather_team(pulled)
    partial_back = collect(pulled_group, slots, adj_vals)
    spread = lax.psum_scatter(partial_back, BLK_AXES, scatter_dimension=0, tiled=True).astype(
        jnp.bfloat16
    )
    grad_input = jnp.dot(spread, weight.T, preferred_element_type=jnp.float32).astype(jnp.bfloat16)
    local_weight = lax.dot_general(
        features, spread, (((0,), (0,)), ((), ())), preferred_element_type=jnp.float32
    )
    local_bias = jnp.sum(pulled.astype(jnp.float32), axis=0)
    both = jnp.concatenate([local_weight, local_bias[None, :]], axis=0)
    both = lax.psum(both, PLANE)
    both = lax.psum(both, ("y_lo", "y_hi", "core"))
    grad_weight = both[:-1]
    grad_bias = both[-1]
    return (hidden, grad_input, grad_weight, grad_bias)


def solution(mesh):
    fine = fine_mesh(mesh)
    rows = P(ALL_AXES, None)
    return jax.shard_map(
        local,
        mesh=fine,
        in_specs=(
            rows,
            P(),
            P(),
            rows,
            P(TEAM_AXES, None, BLK_AXES, None),
            P(TEAM_AXES, None, BLK_AXES, None, None, None),
        ),
        out_specs=(rows, rows, P(), P()),
        check_vma=False,
    )
```

profile of v0, /device:TPU:1, one launch (start us, length us, event | category | flops | bytes accessed | tf_op | source)
XLA Modules:
  0.0 590.6 jit_solution(9726838023997011577)
XLA Ops:
  7.2 1.2 convolution_convert_fusion.1
  8.5 8.3 %collective-permute-start = (bf16[128,256]{1,0:T(8,128)(2,1)S(1)}, bf16[128,256]{1,0:T(8,128)(2,1)S(1)}, u32[]{:S(2)}, u32[]{:S(2)}) collective-permute-start(bf16[128,256]{1,0:T(8,128)(2,1)S(1)} %convolution_convert_fusion.1), channel_id=1, source_target_pairs={{0,32},{32,0},{1,33},{33,1},{2,34},{34,2},{3,35},{35,3},{4,36},{36... | collective-permute-start | bytes 196616 | tf_op jit(solution)/shard_map/ppermute | solution.py:21
  16.8 1.7 collective-permute-done
  18.5 0.7 pad_maximum_fusion.1
  19.2 0.7 compare_and_fusion
  20.0 91.1 %all-gather.3.cloned.1.call-done = bf16[64,128,256]{2,1,0:T(8,128)(2,1)} async-done(((bf16[2,128,256]{2,1,0:T(8,128)(2,1)}), bf16[64,128,256]{2,1,0:T(8,128)(2,1)}) %all-gather.3.cloned.1.call-update) | async-done | bytes 4194320 | tf_op jit(solution)/shard_map/all_gather | solution.py:23
  111.1 8.2 %gather_fusion = bf16[96,128,256]{2,1,0:T(8,128)(2,1)} fusion(bf16[64,128,256]{2,1,0:T(8,128)(2,1)} %all-gather.3.cloned.1.call-done, s32[1024]{0:T(1024)S(1)} %pad_clamp_fusion), kind=kCustom, calls=%fused_computation.clone | custom fusion | bytes 12583296 | tf_op jit(solution)/shard_map/jit(_take)/gather | solution.py:36
  119.3 5.2 fusion.2
  124.6 38.0 %reduce-scatter.3.cloned.1.call-done = f32[128,256]{1,0:T(8,128)} async-done(((f32[1024,256]{1,0:T(8,128)}), f32[128,256]{1,0:T(8,128)}) %reduce-scatter.3.cloned.1.call-update) | async-done | bytes 131088 | tf_op jit(solution)/shard_map/reduce_scatter | solution.py:53
  162.5 1.6 convert_reduce_fusion
  164.2 5.5 collective-permute-start.1
  169.6 3.7 collective-permute-done.1
  173.3 0.7 pad_maximum_fusion.2
  174.1 86.9 %all-gather.5.cloned.1.call-done = bf16[64,128,256]{2,1,0:T(8,128)(2,1)} async-done(((bf16[2,128,256]{2,1,0:T(8,128)(2,1)}), bf16[64,128,256]{2,1,0:T(8,128)(2,1)}) %all-gather.5.cloned.1.call-update) | async-done | bytes 4194320 | tf_op jit(solution)/shard_map/all_gather | solution.py:23
  260.9 8.2 %gather_fusion.1 = bf16[96,128,256]{2,1,0:T(8,128)(2,1)} fusion(bf16[64,128,256]{2,1,0:T(8,128)(2,1)} %all-gather.5.cloned.1.call-done, s32[1024]{0:T(1024)S(1)} %pad_clamp_fusion), kind=kCustom, calls=%fused_computation.1.clone | custom fusion | bytes 12583296 | tf_op jit(solution)/shard_map/jit(_take)/gather | solution.py:36
  269.1 5.2 fusion
  274.4 38.0 %reduce-scatter.5.cloned.1.call-done = f32[128,256]{1,0:T(8,128)} async-done(((f32[1024,256]{1,0:T(8,128)}), f32[128,256]{1,0:T(8,128)}) %reduce-scatter.5.cloned.1.call-update) | async-done | bytes 131088 | tf_op jit(solution)/shard_map/reduce_scatter | solution.py:60
  312.3 1.1 convolution_bitcast_fusion
  313.5 0.7 pad_maximum_fusion
  314.3 153.2 %all-reduce.3.cloned.1.call-done = f32[257,256]{1,0:T(8,128)} async-done(((f32[257,256]{1,0:T(8,128)}), f32[257,256]{1,0:T(8,128)}) %all-reduce.3.cloned.1.call-update) | async-done | bytes 263184 | tf_op jit(solution)/shard_map/psum | solution.py:69
  467.5 1.7 convolution_convert_fusion
  469.2 111.6 %all-reduce.5.cloned.1.call-done = f32[257,256]{1,0:T(8,128)} async-done(((f32[257,256]{1,0:T(8,128)}), f32[257,256]{1,0:T(8,128)}) %all-reduce.5.cloned.1.call-update) | async-done | bytes 263184 | tf_op jit(solution)/shard_map/psum | solution.py:70
  580.8 1.3 slice.13
  582.1 1.7 slice.12
  (24 shorter events, 0.5 us)
Async XLA Ops:
  7.2 112.1 %copy-start = (bf16[1,8,1,12,128,128]{5,4,3,2,1,0:T(8,128)(2,1)S(1)}, bf16[1,8,1,12,128,128]{5,4,3,2,1,0:T(8,128)(2,1)}, u32[]{:S(2)}) copy-start(bf16[1,8,1,12,128,128]{5,4,3,2,1,0:T(8,128)(2,1)} %param.13) | copy-start | bytes 9437188
  7.2 103.9 %all-gather.3.cloned.1.call-start = ((), (), s32[]{:S(2)}) async-start(), calls=%async_computation.2 | async-start | bytes 4325376 | tf_op jit(solution)/shard_map/all_gather | solution.py:23
  8.5 10.0 %collective-permute-start = (bf16[128,256]{1,0:T(8,128)(2,1)S(1)}, bf16[128,256]{1,0:T(8,128)(2,1)S(1)}, u32[]{:S(2)}, u32[]{:S(2)}) collective-permute-start(bf16[128,256]{1,0:T(8,128)(2,1)S(1)} %convolution_convert_fusion.1), channel_id=1, source_target_pairs={{0,32},{32,0},{1,33},{33,1},{2,34},{34,2},{3,35},{35,3},{4,36},{36... | collective-permute-start | bytes 196616 | tf_op jit(solution)/shard_map/ppermute | solution.py:21
  19.2 143.4 %reduce-scatter.3.cloned.1.call-start = ((), (), s32[]{:S(2)}) async-start(), calls=%async_computation.3 | async-start | bytes 1179648 | tf_op jit(solution)/shard_map/reduce_scatter | solution.py:53
  119.3 43.2 %copy-start.3 = (bf16[128,256]{1,0:T(8,128)(2,1)S(1)}, bf16[128,256]{1,0:T(8,128)(2,1)}, u32[]{:S(2)}) copy-start(bf16[128,256]{1,0:T(8,128)(2,1)} %param.11) | copy-start | bytes 196612
  119.3 43.2 %copy-start.4 = (f32[256]{0:T(256)S(1)}, f32[256]{0:T(256)}, u32[]{:S(2)}) copy-start(f32[256]{0:T(256)} %param.10) | copy-start | bytes 3076
  124.5 136.4 %all-gather.5.cloned.1.call-start = ((), (), s32[]{:S(2)}) async-start(), calls=%async_computation.4 | async-start | bytes 4325376 | tf_op jit(solution)/shard_map/all_gather | solution.py:23
  164.2 9.1 %collective-permute-start.1 = (bf16[128,256]{1,0:T(8,128)(2,1)S(1)}, bf16[128,256]{1,0:T(8,128)(2,1)S(1)}, u32[]{:S(2)}, u32[]{:S(2)}) collective-permute-start(bf16[128,256]{1,0:T(8,128)(2,1)S(1)} %get-tuple-element.6), channel_id=1, source_target_pairs={{0,32},{32,0},{1,33},{33,1},{2,34},{34,2},{3,35},{35,3},{4,36},{36... | collective-permute-start | bytes 196616 | tf_op jit(solution)/shard_map/ppermute | solution.py:21
  174.0 138.3 %reduce-scatter.5.cloned.1.call-start = ((), (), s32[]{:S(2)}) async-start(), calls=%async_computation.5 | async-start | bytes 1179648 | tf_op jit(solution)/shard_map/reduce_scatter | solution.py:60
  269.1 43.2 %copy-start.2 = (bf16[128,256]{1,0:T(8,128)(2,1)S(1)}, bf16[128,256]{1,0:T(8,128)(2,1)}, u32[]{:S(2)}) copy-start(bf16[128,256]{1,0:T(8,128)(2,1)} %param.8) | copy-start | bytes 196612
  269.1 198.3 %copy-start.1 = (bf16[256,256]{1,0:T(8,128)(2,1)S(1)}, bf16[256,256]{1,0:T(8,128)(2,1)}, u32[]{:S(2)}) copy-start(bf16[256,256]{1,0:T(8,128)(2,1)} %param.9) | copy-start | bytes 393220
  274.3 193.1 %all-reduce.3.cloned.1.call-start = ((), (), s32[]{:S(2)}) async-start(), calls=%async_computation.6 | async-start | bytes 540672 | tf_op jit(solution)/shard_map/psum | solution.py:69
  314.2 266.6 %all-reduce.5.cloned.1.call-start = ((), (), s32[]{:S(2)}) async-start(), calls=%async_computation.7 | async-start | bytes 540672 | tf_op jit(solution)/shard_map/psum | solution.py:70
Sparse Core Ops, SparseCore 0:
  19.3 91.7 all-gather.2
  124.6 37.8 reduce-scatter.2
  174.1 86.7 all-gather.4
  274.5 37.8 reduce-scatter.4
  315.6 151.7 all-reduce.2
  469.6 111.1 all-reduce.4
where the time goes:
time: 591 us
  waiting for transfers between devices  524 us (89%)
  local copies, waits for them, and re-layouts  19.4 us (3%)
  matrix products  14.5 us (2%)
  between operations  14.2 us (2%)
  starting transfers between devices  14 us (2%)
    all_gather x2, waiting for transfers between devices, gather_team(): full = lax.all_gather(pair, PLANE, axis=0, tiled=True)  178 us
    psum x1, waiting for transfers between devices, local(): both = lax.psum(both, PLANE)  153 us
    psum x1, waiting for transfers between devices, local(): both = lax.psum(both, ('y_lo', 'y_hi', 'core'))  112 us
    reduce_scatter x1, waiting for transfers between devices, local(): lax.psum_scatter(partial_back, BLK_AXES, scatter_dimension=0, tiled=True)  38 us
    reduce_scatter x1, waiting for transfers between devices, local(): lax.psum_scatter(partial_rows, BLK_AXES, scatter_dimension=0, tiled=True)  38 us
    gather x2, local copies, waits for them, and re-layouts, collect(): picked = jnp.take(stacked, slots, axis=0)  16.4 us
    ppermute x2, starting transfers between devices, gather_team(): other = lax.ppermute(rows, 'y_hi', perm=[(0, 1), (1, 0)])  13.7 us
  transfers between devices with their start and end apart: 8, of which 8 were waited for; matrix products, arithmetic and copies ran while one was open for 0% of the time, Pallas kernels for 0%

commit v1 on v0

--- a/solution.py
+++ b/solution.py
@@ -3,6 +3,7 @@
 from jax import lax
 from jax.sharding import Mesh
 from jax.sharding import PartitionSpec as P
+from jax.lax import all_gather
 
 BLK_AXES = ("y_lo", "core")
 TEAM_AXES = ("y_hi", "x", "z")
@@ -66,7 +67,7 @@
     )
     local_bias = jnp.sum(pulled.astype(jnp.float32), axis=0)
     both = jnp.concatenate([local_weight, local_bias[None, :]], axis=0)
-    both = lax.psum(both, PLANE)
+    both = all_gather(both, PLANE).sum(axis=0)
     both = lax.psum(both, ("y_lo", "y_hi", "core"))
     grad_weight = both[:-1]
     grad_bias = both[-1]

time: 591 us -> 544 us (0.920)
  waiting for transfers between devices: 524 us -> 473 us
    psum x1 -> x0, waiting for transfers between devices: 153 us -> none  [local(): both = lax.psum(both, PLANE)]
    all_gather x0 -> x1, waiting for transfers between devices: none -> 107 us  [local(): both = all_gather(both, PLANE).sum(axis=0)]
where the time goes in v1:
time: 544 us
  waiting for transfers between devices  473 us (87%)
  local copies, waits for them, and re-layouts  19.4 us (4%)
  starting transfers between devices  14.3 us (3%)
  between operations  14.2 us (3%)
  matrix products  13.7 us (3%)
  other arithmetic  9.19 us (2%)
    all_gather x2, waiting for transfers between devices, gather_team(): full = lax.all_gather(pair, PLANE, axis=0, tiled=True)  178 us
    all_gather x1, waiting for transfers between devices, local(): both = all_gather(both, PLANE).sum(axis=0)  107 us
    psum x1, waiting for transfers between devices, local(): both = lax.psum(both, ('y_lo', 'y_hi', 'core'))  107 us
    reduce_scatter x1, waiting for transfers between devices, local(): lax.psum_scatter(partial_rows, BLK_AXES, scatter_dimension=0, tiled=True)  37.9 us
    reduce_scatter x1, waiting for transfers between devices, local(): lax.psum_scatter(partial_back, BLK_AXES, scatter_dimension=0, tiled=True)  37.9 us
    gather x2, local copies, waits for them, and re-layouts, collect(): picked = jnp.take(stacked, slots, axis=0)  16.4 us
    ppermute x2, starting transfers between devices, gather_team(): other = lax.ppermute(rows, 'y_hi', perm=[(0, 1), (1, 0)])  14.1 us
  transfers between devices with their start and end apart: 8, of which 8 were waited for; matrix products, arithmetic and copies ran while one was open for 0% of the time, Pallas kernels for 0%

profile of v1, /device:TPU:1, one launch (start us, length us, event | category | flops | bytes accessed | tf_op | source)
XLA Modules:
  0.0 543.8 jit_solution(10497180695089417400)
XLA Ops:
  7.2 1.2 convolution_convert_fusion.1
  8.5 8.3 %collective-permute-start = (bf16[128,256]{1,0:T(8,128)(2,1)S(1)}, bf16[128,256]{1,0:T(8,128)(2,1)S(1)}, u32[]{:S(2)}, u32[]{:S(2)}) collective-permute-start(bf16[128,256]{1,0:T(8,128)(2,1)S(1)} %convolution_convert_fusion.1), channel_id=1, source_target_pairs={{0,32},{32,0},{1,33},{33,1},{2,34},{34,2},{3,35},{35,3},{4,36},{36... | collective-permute-start | bytes 196616 | tf_op jit(solution)/shard_map/ppermute | solution.py:22
  16.8 1.7 collective-permute-done
  18.5 0.7 pad_maximum_fusion
  19.2 0.7 compare_and_fusion
  20.0 91.1 %all-gather.6.cloned.1.call-done = bf16[64,128,256]{2,1,0:T(8,128)(2,1)} async-done(((bf16[2,128,256]{2,1,0:T(8,128)(2,1)}), bf16[64,128,256]{2,1,0:T(8,128)(2,1)}) %all-gather.6.cloned.1.call-update) | async-done | bytes 4194320 | tf_op jit(solution)/shard_map/all_gather | solution.py:24
  111.1 8.2 %gather_fusion = bf16[96,128,256]{2,1,0:T(8,128)(2,1)} fusion(bf16[64,128,256]{2,1,0:T(8,128)(2,1)} %all-gather.6.cloned.1.call-done, s32[1024]{0:T(1024)S(1)} %pad_clamp_fusion), kind=kCustom, calls=%fused_computation.clone | custom fusion | bytes 12583296 | tf_op jit(solution)/shard_map/jit(_take)/gather | solution.py:37
  119.3 5.2 fusion.2
  124.6 37.9 %reduce-scatter.3.cloned.1.call-done = f32[128,256]{1,0:T(8,128)} async-done(((f32[1024,256]{1,0:T(8,128)}), f32[128,256]{1,0:T(8,128)}) %reduce-scatter.3.cloned.1.call-update) | async-done | bytes 131088 | tf_op jit(solution)/shard_map/reduce_scatter | solution.py:54
  162.5 1.6 convert_reduce_fusion
  164.1 5.8 %collective-permute-start.1 = (bf16[128,256]{1,0:T(8,128)(2,1)S(1)}, bf16[128,256]{1,0:T(8,128)(2,1)S(1)}, u32[]{:S(2)}, u32[]{:S(2)}) collective-permute-start(bf16[128,256]{1,0:T(8,128)(2,1)S(1)} %get-tuple-element.6), channel_id=1, source_target_pairs={{0,32},{32,0},{1,33},{33,1},{2,34},{34,2},{3,35},{35,3},{4,36},{36... | collective-permute-start | bytes 196616 | tf_op jit(solution)/shard_map/ppermute | solution.py:22
  170.0 3.4 collective-permute-done.1
  174.1 86.8 %all-gather.8.cloned.1.call-done = bf16[64,128,256]{2,1,0:T(8,128)(2,1)} async-done(((bf16[2,128,256]{2,1,0:T(8,128)(2,1)}), bf16[64,128,256]{2,1,0:T(8,128)(2,1)}) %all-gather.8.cloned.1.call-update) | async-done | bytes 4194320 | tf_op jit(solution)/shard_map/all_gather | solution.py:24
  260.9 8.2 %gather_fusion.1 = bf16[96,128,256]{2,1,0:T(8,128)(2,1)} fusion(bf16[64,128,256]{2,1,0:T(8,128)(2,1)} %all-gather.8.cloned.1.call-done, s32[1024]{0:T(1024)S(1)} %pad_clamp_fusion), kind=kCustom, calls=%fused_computation.1.clone | custom fusion | bytes 12583296 | tf_op jit(solution)/shard_map/jit(_take)/gather | solution.py:37
  269.1 5.2 fusion
  274.4 37.9 %reduce-scatter.5.cloned.1.call-done = f32[128,256]{1,0:T(8,128)} async-done(((f32[1024,256]{1,0:T(8,128)}), f32[128,256]{1,0:T(8,128)}) %reduce-scatter.5.cloned.1.call-update) | async-done | bytes 131088 | tf_op jit(solution)/shard_map/reduce_scatter | solution.py:61
  312.3 1.2 convolution_bitcast_fusion
  313.5 0.7 maximum_bitcast_fusion
  314.3 107.4 %all-gather.10.cloned.1.call-done = f32[32,257,256]{2,1,0:T(8,128)} async-done(((f32[1,257,256]{2,1,0:T(8,128)}), f32[32,257,256]{2,1,0:T(8,128)}) %all-gather.10.cloned.1.call-update) | async-done | bytes 8421392 | tf_op jit(solution)/shard_map/all_gather | solution.py:70
  421.7 4.7 reduce_sum.19
  426.5 0.8 convolution_convert_fusion
  427.4 106.6 %all-reduce.2.cloned.1.call-done = f32[257,256]{1,0:T(8,128)} async-done(((f32[257,256]{1,0:T(8,128)}), f32[257,256]{1,0:T(8,128)}) %all-reduce.2.cloned.1.call-update) | async-done | bytes 263184 | tf_op jit(solution)/shard_map/psum | solution.py:71
  534.0 1.3 slice.13
  535.3 1.7 slice.12
  (27 shorter events, 1.1 us)
Async XLA Ops:
  7.2 112.1 %copy-start = (bf16[1,8,1,12,128,128]{5,4,3,2,1,0:T(8,128)(2,1)S(1)}, bf16[1,8,1,12,128,128]{5,4,3,2,1,0:T(8,128)(2,1)}, u32[]{:S(2)}) copy-start(bf16[1,8,1,12,128,128]{5,4,3,2,1,0:T(8,128)(2,1)} %param.13) | copy-start | bytes 9437188
  7.2 103.9 %all-gather.6.cloned.1.call-start = ((), (), s32[]{:S(2)}) async-start(), calls=%async_computation.2 | async-start | bytes 4325376 | tf_op jit(solution)/shard_map/all_gather | solution.py:24
  8.5 10.0 %collective-permute-start = (bf16[128,256]{1,0:T(8,128)(2,1)S(1)}, bf16[128,256]{1,0:T(8,128)(2,1)S(1)}, u32[]{:S(2)}, u32[]{:S(2)}) collective-permute-start(bf16[128,256]{1,0:T(8,128)(2,1)S(1)} %convolution_convert_fusion.1), channel_id=1, source_target_pairs={{0,32},{32,0},{1,33},{33,1},{2,34},{34,2},{3,35},{35,3},{4,36},{36... | collective-permute-start | bytes 196616 | tf_op jit(solution)/shard_map/ppermute | solution.py:22
  19.2 143.3 %reduce-scatter.3.cloned.1.call-start = ((), (), s32[]{:S(2)}) async-start(), calls=%async_computation.3 | async-start | bytes 1179648 | tf_op jit(solution)/shard_map/reduce_scatter | solution.py:54
  119.3 43.2 %copy-start.4 = (bf16[128,256]{1,0:T(8,128)(2,1)S(1)}, bf16[128,256]{1,0:T(8,128)(2,1)}, u32[]{:S(2)}) copy-start(bf16[128,256]{1,0:T(8,128)(2,1)} %param.11) | copy-start | bytes 196612
  119.3 43.2 %copy-start.5 = (f32[256]{0:T(256)S(1)}, f32[256]{0:T(256)}, u32[]{:S(2)}) copy-start(f32[256]{0:T(256)} %param.10) | copy-start | bytes 3076
  124.5 136.4 %all-gather.8.cloned.1.call-start = ((), (), s32[]{:S(2)}) async-start(), calls=%async_computation.4 | async-start | bytes 4325376 | tf_op jit(solution)/shard_map/all_gather | solution.py:24
  164.1 9.3 %collective-permute-start.1 = (bf16[128,256]{1,0:T(8,128)(2,1)S(1)}, bf16[128,256]{1,0:T(8,128)(2,1)S(1)}, u32[]{:S(2)}, u32[]{:S(2)}) collective-permute-start(bf16[128,256]{1,0:T(8,128)(2,1)S(1)} %get-tuple-element.6), channel_id=1, source_target_pairs={{0,32},{32,0},{1,33},{33,1},{2,34},{34,2},{3,35},{35,3},{4,36},{36... | collective-permute-start | bytes 196616 | tf_op jit(solution)/shard_map/ppermute | solution.py:22
  174.1 138.2 %reduce-scatter.5.cloned.1.call-start = ((), (), s32[]{:S(2)}) async-start(), calls=%async_computation.5 | async-start | bytes 1179648 | tf_op jit(solution)/shard_map/reduce_scatter | solution.py:61
  269.1 43.2 %copy-start.3 = (bf16[128,256]{1,0:T(8,128)(2,1)S(1)}, bf16[128,256]{1,0:T(8,128)(2,1)}, u32[]{:S(2)}) copy-start(bf16[128,256]{1,0:T(8,128)(2,1)} %param.8) | copy-start | bytes 196612
  274.3 152.2 %copy-start.2 = (bf16[256,256]{1,0:T(8,128)(2,1)S(1)}, bf16[256,256]{1,0:T(8,128)(2,1)}, u32[]{:S(2)}) copy-start(bf16[256,256]{1,0:T(8,128)(2,1)} %param.9) | copy-start | bytes 393220
  274.3 147.4 %all-gather.10.cloned.1.call-start = ((), (), s32[]{:S(2)}) async-start(), calls=%async_computation.7 | async-start | bytes 8921088 | tf_op jit(solution)/shard_map/all_gather | solution.py:70
  312.3 114.2 %copy-start.1 = (f32[128,256]{1,0:T(8,128)S(1)}, f32[128,256]{1,0:T(8,128)}, u32[]{:S(2)}) copy-start(f32[128,256]{1,0:T(8,128)} %reduce-scatter.5.cloned.1.call-done) | copy-start | bytes 393220
  314.2 219.8 %all-reduce.2.cloned.1.call-start = ((), (), s32[]{:S(2)}) async-start(), calls=%async_computation.6 | async-start | bytes 540672 | tf_op jit(solution)/shard_map/psum | solution.py:71
Sparse Core Ops, SparseCore 0:
  19.3 91.7 all-gather.5
  124.7 37.7 reduce-scatter.2
  174.2 86.6 all-gather.7
  274.4 37.7 reduce-scatter.4
  315.3 106.4 all-gather.9
  426.6 107.3 all-reduce.1
